TPU v7x, 512 devices: a whole 4x4x16 slice. The times are simulated.
512 devices in a mesh: vox: 8 (over z_lo), frm: 64 (over z_hi, y, x, core).
Axes of the slice: x: 4, y: 4, z: 16 (z_hi: 2, z_lo: 8; z = z_hi * 8 + z_lo), core: 2. Of those that a mesh axis runs over, the one named last changes fastest.
Arguments:
- spatial_coeffs: bfloat16 [2, 32, 256, 256], P(None, None, 'vox'), may hold values from -15 to 15
- temporal_basis: bfloat16 [32, 512], P(None, 'frm'), may hold values from -0.25 to 0.25
- coil_maps: bfloat16 [2, 4, 256, 256], P(None, None, 'vox'), may hold values from -4 to 4
- line_index: int32 [512, 8], P('frm'), may hold values from 0 to 255
- kspace_data: bfloat16 [512, 4, 2, 8, 256], P('frm', None, None, None, 'vox'), may hold values from -6 to 6
Outputs:
- coeff_grad: float32 [256, 2, 32, 256], P('frm', None, None, 'vox')
- basis_grad: float32 [32, 512], P(None, 'frm')
Inputs may be any that keep to these rules, and one draw needn't show every extreme that they name: `line_index`: line numbers are drawn independently; a line may be sampled twice in one frame.
All inputs are finite; a program needn't handle non-finite values.
Results may differ from a plain program's by a relative error of at most 0.012.
Values may be sent and summed in bfloat16 or wider, within the bound.
No kernel may reach another device: no remote copies, remote signals or barrier semaphores. Data moves between devices by JAX's collectives and lax.ppermute only.
A program may use at most 64 MiB of HBM per device.

v0:
```python
import math

import jax
import jax.numpy as jnp
from jax import lax
from jax.sharding import PartitionSpec as P


def dft_table(length):
    indices = jnp.arange(length, dtype=jnp.int32)
    phases = indices[:, None] * indices[None, :] % length
    angles = phases.astype(jnp.float32) * (2.0 * math.pi / length)
    factor = 1.0 / math.sqrt(length)
    cosine = (jnp.cos(angles) * factor).astype(jnp.bfloat16)
    sine = (-jnp.sin(angles) * factor).astype(jnp.bfloat16)
    top_half = jnp.concatenate([cosine, sine], axis=1)
    low_half = jnp.concatenate([-sine, cosine], axis=1)
    return jnp.concatenate([top_half, low_half], axis=0)


def line_tables(line_index, row_numbers, height):
    phases = line_index[:, :, None] * row_numbers[None, None, :] % height
    angles = phases.astype(jnp.float32) * (2.0 * math.pi / height)
    factor = 1.0 / math.sqrt(height)
    cosine = (jnp.cos(angles) * factor).astype(jnp.bfloat16)
    sine = (-jnp.sin(angles) * factor).astype(jnp.bfloat16)
    return jnp.stack([cosine, sine], axis=1)


def line_forward(tables, hybrid):
    product = jnp.einsum("tajr,tcrbk->tcajbk", tables, hybrid, preferred_element_type=jnp.float32)
    part_real = product[:, :, 0, :, 0] - product[:, :, 1, :, 1]
    part_imag = product[:, :, 0, :, 1] + product[:, :, 1, :, 0]
    return jnp.stack([part_real, part_imag], axis=2)


def line_adjoint(tables, residual):
    product = jnp.einsum("tajr,tcbjk->tcrabk", tables, residual, preferred_element_type=jnp.float32)
    part_real = product[:, :, :, 0, 0] + product[:, :, :, 1, 1]
    part_imag = product[:, :, :, 0, 1] - product[:, :, :, 1, 0]
    return jnp.stack([part_real, part_imag], axis=3).astype(jnp.bfloat16)


def local(spatial_coeffs, temporal_basis, coil_maps, line_index, kspace_data):
    row_count = spatial_coeffs.shape[2]
    col_count = spatial_coeffs.shape[3]
    frames = temporal_basis.shape[1]
    coil_count = coil_maps.shape[1]
    height = row_count * lax.axis_size("vox")
    table_full = dft_table(col_count)
    images = jnp.einsum(
        "plrx,lt->tprx", spatial_coeffs, temporal_basis, preferred_element_type=jnp.float32
    )
    map_real = coil_maps[0].astype(jnp.float32)[None]
    map_imag = coil_maps[1].astype(jnp.float32)[None]
    img_real = images[:, 0][:, None]
    img_imag = images[:, 1][:, None]
    coil_real = map_real * img_real - map_imag * img_imag
    coil_imag = map_real * img_imag + map_imag * img_real
    coil_images = jnp.concatenate([coil_real, coil_imag], axis=-1).astype(jnp.bfloat16)
    hybrid = jnp.dot(coil_images, table_full, preferred_element_type=jnp.float32).astype(
        jnp.bfloat16
    )
    hybrid = hybrid.reshape(frames, coil_count, row_count, 2, col_count)
    measured = kspace_data.astype(jnp.float32)
    row_numbers = lax.axis_index("vox") * row_count + jnp.arange(row_count, dtype=jnp.int32)
    tables = line_tables(line_index, row_numbers, height)
    partial_value = line_forward(tables, hybrid)
    predicted = lax.psum_scatter(
        partial_value.astype(jnp.bfloat16), "vox", scatter_dimension=4, tiled=True
    ).astype(jnp.float32)
    residual = (predicted - measured).astype(jnp.bfloat16)
    residual = lax.all_gather(residual, "vox", axis=4, tiled=True)
    back_hybrid = line_adjoint(tables, residual)
    back_hybrid = back_hybrid.reshape(frames, coil_count, row_count, 2 * col_count)
    adjoint = jnp.dot(back_hybrid, table_full.T, preferred_element_type=jnp.float32)
    adj_real = adjoint[..., :col_count]
    adj_imag = adjoint[..., col_count:]
    grad_real = jnp.sum(map_real * adj_real + map_imag * adj_imag, axis=1)
    grad_imag = jnp.sum(map_real * adj_imag - map_imag * adj_real, axis=1)
    frame_grad = jnp.stack([grad_real, grad_imag], axis=1).astype(jnp.bfloat16)
    basis_term = jnp.einsum(
        "plrx,tprx->lt", spatial_coeffs, frame_grad, preferred_element_type=jnp.float32
    )
    basis_grad = lax.psum(basis_term, "vox") / height
    coeff_grad = lax.psum_scatter(
        jnp.einsum("tprx,lt->xplr", frame_grad, temporal_basis, preferred_element_type=jnp.float32),
        "frm",
        scatter_dimension=0,
        tiled=True,
    )
    return (coeff_grad, basis_grad)


def solution(mesh):
    placed = (
        P(None, None, "vox", None),
        P(None, "frm"),
        P(None, None, "vox", None),
        P("frm", None),
        P("frm", None, None, None, "vox"),
    )
    return jax.shard_map(
        local,
        mesh=mesh,
        in_specs=placed,
        out_specs=(P("frm", None, None, "vox"), P(None, "frm")),
        check_vma=False,
    )
```

profile of v0, /device:TPU:31, one launch (start us, length us, event | category | flops | bytes accessed | tf_op | source)
XLA Modules:
  0.0 804.6 jit_solution(15970291774516055137)
XLA Ops:
  7.2 0.0 copy-start
  7.2 0.0 reduce-scatter.7.cloned.1.call-start
  7.2 1.0 fusion.31
  8.2 1.1 multiply_convert_fusion
  9.3 0.0 copy-start.2
  9.3 0.0 copy-start.4
  9.4 1.0 bitcast_convert_fusion.1
  10.3 0.0 copy-done
  10.4 1.3 fusion.13
  11.7 0.1 copy.33
  11.8 0.1 copy.34
  11.9 0.0 copy-start.7
  11.9 0.3 subtract_convert_fusion
  12.2 0.0 copy-done.2
  12.2 0.0 copy-done.4
  12.3 0.7 convolution_convert_fusion
  13.0 0.3 reshape.154
  13.3 0.0 copy-done.7
  13.3 0.2 multiply_convert_fusion.3
  13.5 0.3 convolution_bitcast_fusion.1
  13.9 0.0 copy-start.1
  13.9 5.4 copy.58
  19.3 7.7 reshape.163
  27.0 0.0 reduce-scatter.7.cloned.1.call-update
  27.0 0.0 reduce-scatter.5.cloned.1.call-start
  27.0 62.5 %reduce-scatter.7.cloned.1.call-done = bf16[32,512]{1,0:T(8,128)(2,1)} async-done(((bf16[256,512]{1,0:T(8,128)(2,1)}), bf16[32,512]{1,0:T(8,128)(2,1)}) %reduce-scatter.7.cloned.1.call-update) | async-done | bytes 32784
  89.5 1.4 reshape.164
  90.9 0.6 copy.59
  91.5 0.0 copy-done.1
  91.6 0.9 copy.39
  92.5 81.2 %all_gather.3 = bf16[8,4,2,8,256]{3,0,2,1,4:T(8,128)(2,1)S(1)} all-gather(bf16[8,4,2,8,32]{3,0,2,1,4:T(8,128)(2,1)S(1)} %copy.39), channel_id=1, replica_groups=mesh['vox'=8,'frm'=64] {'vox'}, dimensions={4}, use_global_device_ids=true | all-gather | bytes 294912 | tf_op jit(solution)/shard_map/all_gather | solution.py:73
  173.6 5.0 fusion.2
  178.6 0.0 copy-start.3
  178.6 0.0 copy-start.5
  178.6 0.2 fusion.16
  178.8 0.2 fusion.15
  179.0 0.1 maximum_bitcast_fusion
  179.1 0.0 copy-start.6
  179.1 0.1 copy.64
  179.2 0.3 copy-done.3
  179.5 0.1 copy-done.5
  179.6 0.7 fusion.17
  180.3 0.3 add_reduce_fusion
  180.6 0.1 copy.82
  180.7 0.1 copy.83
  180.8 0.0 copy-done.6
  180.8 0.5 convolution_bitcast_fusion
  181.3 7.6 copy.46
  188.8 0.0 reduce-scatter.5.cloned.1.call-update
  188.8 0.7 convolution_bitcast_fusion.2
  189.5 26.4 %psum.7 = f32[32,8]{0,1:T(8,128)S(1)} all-reduce(f32[32,8]{0,1:T(8,128)S(1)} %convolution_bitcast_fusion.2), channel_id=1, replica_groups=mesh['vox'=8,'frm'=64] {'vox'}, use_global_device_ids=true, to_apply=%region_4.5 | all-reduce | flops 256 | bytes 2048 | tf_op jit(solution)/shard_map/psum | solution.py:85
  216.0 0.6 broadcast_multiply_fusion
  216.6 581.2 %reduce-scatter.5.cloned.1.call-done = f32[4,2,32,32]{3,2,1,0:T(8,128)} async-done(((f32[256,2,32,32]{3,2,1,0:T(8,128)}), f32[4,2,32,32]{3,2,1,0:T(8,128)}) %reduce-scatter.5.cloned.1.call-update) | async-done | bytes 32784 | tf_op jit(solution)/shard_map/reduce_scatter | solution.py:86
  (6 shorter events, 0.2 us)
Async XLA Ops:
  7.2 3.2 copy-start
  7.2 82.3 %reduce-scatter.7.cloned.1.call-start = ((), (), s32[]{:S(2)}) async-start(), calls=%async_computation.3 | async-start | bytes 294912
  9.3 2.9 copy-start.2
  9.3 2.9 copy-start.4
  11.9 1.3 copy-start.7
  13.9 77.6 %copy-start.1 = (bf16[8,4,2,8,32]{4,3,2,1,0:T(8,128)(2,1)S(1)}, bf16[8,4,2,8,32]{4,3,2,1,0:T(8,128)(2,1)}, u32[]{:S(2)}) copy-start(bf16[8,4,2,8,32]{4,3,2,1,0:T(8,128)(2,1)} %param.9) | copy-start | bytes 98308
  27.0 770.8 %reduce-scatter.5.cloned.1.call-start = ((), (), s32[]{:S(2)}) async-start(), calls=%async_computation.2 | async-start | bytes 8519680 | tf_op jit(solution)/shard_map/reduce_scatter | solution.py:86
  178.6 0.9 copy-start.3
  178.6 1.0 copy-start.5
  179.1 1.7 copy-start.6
Sparse Core Ops, SparseCore 0:
  27.1 62.3 reduce-scatter.6
  189.0 608.7 reduce-scatter.4
where the time goes:
time: 805 us
  waiting for transfers between devices  644 us (80%)
  blocking collectives  108 us (13%)
  local copies, waits for them, and re-layouts  24.7 us (3%)
  between operations  14.3 us (2%)
  matrix products  9.21 us (1%)
    reduce_scatter x1, waiting for transfers between devices, local(): lax.psum_scatter(jnp.einsum('tprx,lt->xplr', frame_grad, temporal_basis,...  581 us
    all_gather x1, blocking collectives, local(): residual = lax.all_gather(residual, 'vox', axis=4, tiled=True)  81.2 us
    unnamed x3, waiting for transfers between devices  62.5 us
    psum x1, blocking collectives, local(): basis_grad = lax.psum(basis_term, 'vox') / height  26.4 us
  transfers between devices with their start and end apart: 2, of which 2 were waited for; matrix products, arithmetic and copies ran while one was open for 0% of the time, Pallas kernels for 0%

commit v1 on v0

v1 whole, which is shorter than its diff:
```python
import math

import jax
import jax.numpy as jnp
import numpy as np
from jax import lax
from jax.experimental import pallas as pl
from jax.experimental.pallas import tpu as pltpu
from jax.sharding import PartitionSpec as P

F32 = jnp.float32
BF16 = jnp.bfloat16
VMEM = pl.BlockSpec(memory_space=pltpu.VMEM)
SMEM = pl.BlockSpec(memory_space=pltpu.SMEM)


def dot_nn(a, b):
    return lax.dot_general(a, b, (((1,), (0,)), ((), ())), preferred_element_type=F32)


def dot_nt(a, b, precision=None):
    return lax.dot_general(
        a, b, (((1,), (1,)), ((), ())), preferred_element_type=F32, precision=precision
    )


def dot_tn(a, b):
    return lax.dot_general(a, b, (((0,), (0,)), ((), ())), preferred_element_type=F32)


def iota(shape, axis):
    return lax.broadcasted_iota(jnp.int32, shape, axis)


def one_hot(condition):
    return jnp.where(condition, 1.0, 0.0).astype(BF16)


def dft_block(length):
    indices = np.arange(length, dtype=np.int64)
    phases = (indices[:, None] * indices[None, :]) % length
    angles = phases.astype(np.float32) * np.float32(2.0 * math.pi / length)
    factor = np.float32(1.0 / math.sqrt(length))
    cosine = np.cos(angles) * factor
    sine = -np.sin(angles) * factor
    top = np.concatenate([cosine, -sine], axis=1)
    low = np.concatenate([sine, cosine], axis=1)
    return np.concatenate([top, low], axis=0).astype(BF16)


def line_blocks(base, frames):
    lane_frame = iota(base.shape, 1) // (base.shape[1] // frames)
    wide = base.astype(F32)
    return jnp.concatenate(
        [jnp.where(lane_frame == t, wide, 0.0).astype(BF16) for t in range(frames)], axis=0
    )


def over_frames(block, frames):
    return jnp.concatenate([block] * frames, axis=0)


def forward_kernel(u_ref, phi_ref, maps_ref, base_a_ref, base_b_ref, dft_ref, out_ref):
    rank, frames = phi_ref.shape[1], phi_ref.shape[0]
    coils, rows, cols = maps_ref.shape[1:]
    lines = base_a_ref.shape[1]
    spread = one_hot(iota((rank, rank * rows), 1) // rows == iota((rank, rank * rows), 0))
    phi_wide = dot_nn(phi_ref[...], spread)
    same_row = iota((rows, rank * rows), 1) % rows == iota((rows, rank * rows), 0)
    mix = jnp.concatenate(
        [
            jnp.where(same_row, jnp.broadcast_to(phi_wide[t : t + 1], same_row.shape), 0.0).astype(BF16)
            for t in range(frames)
        ],
        axis=0,
    )
    img_real = dot_nn(mix, u_ref[0])
    img_imag = dot_nn(mix, u_ref[1])
    sampling = jnp.concatenate(
        [line_blocks(base_a_ref[...], frames), line_blocks(base_b_ref[...], frames)], axis=0
    )
    for c in range(coils):
        map_real = over_frames(maps_ref[0, c].astype(F32), frames)
        map_imag = over_frames(maps_ref[1, c].astype(F32), frames)
        coil_real = (map_real * img_real - map_imag * img_imag).astype(BF16)
        coil_imag = (map_real * img_imag + map_imag * img_real).astype(BF16)
        coil = jnp.concatenate([coil_real, coil_imag], axis=1)
        hybrid = dot_nt(dft_ref[...], coil).astype(BF16)
        hybrid = jnp.concatenate([hybrid[:cols], hybrid[cols:]], axis=1)
        out_ref[:, c * lines : (c + 1) * lines] = dot_nn(hybrid, sampling).astype(BF16)


def residual_kernel(parts_ref, data_ref, out_ref):
    members, span, width = parts_ref.shape
    total = parts_ref[0].astype(F32)
    for m in range(1, members):
        total = total + parts_ref[m].astype(F32)
    frames, coils, group = data_ref.shape[0], data_ref.shape[1], data_ref.shape[2]
    data = jnp.concatenate(
        [data_ref[t, c] for c in range(coils) for t in range(frames)], axis=0
    )
    eye = one_hot(iota((span, span), 0) == iota((span, span), 1))
    residual = (total - dot_nt(eye, data)).astype(BF16)
    for m in range(members):
        out_ref[m] = residual


def backward_kernel(
    with_phi, offset_ref, res_ref, u_ref, phi_ref, maps_ref, base_a_ref, base_b_ref, dft_ref,
    out_ref, basis_ref,
):
    rank, frames = phi_ref.shape[1], phi_ref.shape[0]
    coils, rows, cols = maps_ref.shape[1:]
    lines = base_a_ref.shape[1]
    half = cols // 2
    offset = pl.multiple_of(offset_ref[0], half)
    here = pl.ds(offset, half)
    there = pl.ds(pl.multiple_of(offset + cols, half), half)
    points = frames * rows
    sampling = jnp.concatenate(
        [line_blocks(base_a_ref[...], frames), line_blocks(base_b_ref[...], frames)], axis=0
    )
    adjoint = jnp.concatenate([dft_ref[:, here], dft_ref[:, there]], axis=1)
    grad_real = jnp.zeros((points, half), F32)
    grad_imag = jnp.zeros((points, half), F32)
    for c in range(coils):
        back = dot_nt(sampling, res_ref[:, c * lines : (c + 1) * lines]).astype(BF16)
        back = jnp.concatenate([back[:points], back[points:]], axis=1)
        adj = dot_nn(back, adjoint)
        adj_real, adj_imag = adj[:, :half], adj[:, half:]
        map_real = over_frames(maps_ref[0, c, :, here].astype(F32), frames)
        map_imag = over_frames(maps_ref[1, c, :, here].astype(F32), frames)
        grad_real = grad_real + (map_real * adj_real + map_imag * adj_imag)
        grad_imag = grad_imag + (map_real * adj_imag - map_imag * adj_real)
    grad_real = grad_real.astype(BF16)
    grad_imag = grad_imag.astype(BF16)
    quads = frames // 2
    places = half * quads
    moved = jnp.zeros((places, 2 * 2 * rows), F32)
    for q in range(quads):
        piece = jnp.concatenate(
            [grad_real[q * 2 * rows : (q + 1) * 2 * rows], grad_imag[q * 2 * rows : (q + 1) * 2 * rows]],
            axis=0,
        )
        chosen = one_hot(iota((places, half), 0) == iota((places, half), 1) * quads + q)
        moved = moved + dot_nt(chosen, piece)
    owners = out_ref.shape[0]
    size = places // owners
    out_ref[:, :size, :] = moved.astype(BF16).reshape(owners, size, 4 * rows)
    if with_phi:
        lanes = 4 * rank
        row, lane = iota((frames, lanes), 0), iota((frames, lanes), 1)
        spread = one_hot(iota((rank, lanes), 1) % rank == iota((rank, lanes), 0))
        phi_wide = dot_nn(phi_ref[...], spread).astype(BF16)
        square = (frames, frames)
        first = dot_nn(one_hot(iota(square, 1) == iota(square, 0) % quads * 2), phi_wide)
        second = dot_nn(one_hot(iota(square, 1) == iota(square, 0) % quads * 2 + 1), phi_wide)
        tile = jnp.where(lane // rank % 2 == 0, first, second)
        tile = jnp.where(lane // (2 * rank) == row // quads, tile, 0.0).astype(BF16)
        for d in range(owners):
            out_ref[d, size:, :] = tile
    both = jnp.concatenate([grad_real, grad_imag], axis=1)
    coeffs = jnp.concatenate([u_ref[0, :, here], u_ref[1, :, here]], axis=1)
    cross = dot_nt(coeffs, both)
    cross = cross.reshape(rank, rows, points)
    keep = iota((rows, points), 1) % rows == iota((rows, points), 0)
    per_rank = jnp.concatenate(
        [
            jnp.sum(jnp.where(keep, cross[l], 0.0), axis=0, keepdims=True)
            for l in range(rank)
        ],
        axis=0,
    )
    frame_sum = jnp.where(
        iota((frames, points), 1) // rows == iota((frames, points), 0), 1.0, 0.0
    )
    basis_ref[...] = dot_nt(frame_sum, per_rank, lax.Precision.HIGHEST)


def combine(parts, weights, rank):
    summed = []
    for h in range(2):
        part = parts[h]
        product = dot_tn(weights, part)
        halves = []
        for x in range(2):
            first = product[(2 * x) * rank : (2 * x + 1) * rank]
            second = product[(2 * x + 1) * rank : (2 * x + 2) * rank]
            halves.append(first + pltpu.roll(second, first.shape[1] - rank, 1))
        summed.append(jnp.concatenate(halves, axis=0))
    lane = iota(summed[0].shape, 1)
    return jnp.where(lane // rank % 2 == 0, summed[0], pltpu.roll(summed[1], rank, 1))


def tiles(ref, first):
    owners, lanes = ref.shape[0], ref.shape[2]
    wide = ref[:, first : first + 8, :].astype(F32)
    return wide.reshape(owners * 8, lanes).astype(BF16)


def far_kernel(a_ref, out_ref):
    rank = 32
    total = combine([tiles(a_ref, 0), tiles(a_ref, 8)], tiles(a_ref, 16), rank)
    out_ref[...] = total.astype(BF16)


def near_kernel(b_ref, a_ref, far_ref, out_ref):
    rank = out_ref.shape[2]
    rows = out_ref.shape[3]
    total = combine([tiles(b_ref, 0), tiles(b_ref, 8)], tiles(a_ref, 16), rank)
    total = total + far_ref[...].astype(F32)
    for h in range(2):
        for x in range(2):
            for p in range(2):
                lane = p * 2 * rows + h * rows
                out_ref[h * 2 + x, p] = total[x * rank : (x + 1) * rank, lane : lane + rows]


def call(kernel, out_shape, specs, flops, bytes_accessed):
    return pl.pallas_call(
        kernel,
        out_shape=out_shape,
        in_specs=specs,
        out_specs=jax.tree.map(lambda _: VMEM, out_shape),
        compiler_params=pltpu.CompilerParams(vmem_limit_bytes=40 * 1024 * 1024),
        cost_estimate=pl.CostEstimate(
            flops=flops, bytes_accessed=bytes_accessed, transcendentals=0
        ),
    )


def shape(dims, dtype):
    return jax.ShapeDtypeStruct(dims, dtype)


def local(spatial_coeffs, temporal_basis, coil_maps, line_index, kspace_data):
    rank, rows, cols = spatial_coeffs.shape[1:]
    frames = temporal_basis.shape[1]
    coils = coil_maps.shape[1]
    lines = line_index.shape[1]
    members = lax.axis_size("vox")
    devices = lax.axis_size("frm")
    owners = devices // 2
    span = kspace_data.shape[4]
    height = rows * members
    lanes = frames * 2 * lines

    dft = jnp.asarray(dft_block(cols))
    u = spatial_coeffs.reshape(2, rank * rows, cols)
    phi = temporal_basis.T
    row_numbers = lax.axis_index("vox") * rows + jnp.arange(rows, dtype=jnp.int32)
    wide_lines = jnp.broadcast_to(line_index[:, None, :], (frames, 2, lines)).reshape(1, lanes)
    phases = wide_lines * row_numbers[:, None] % height
    angles = phases.astype(F32) * (2.0 * math.pi / height)
    factor = 1.0 / math.sqrt(height)
    cosine = jnp.cos(angles) * factor
    sine = -jnp.sin(angles) * factor
    is_real = (jnp.arange(lanes, dtype=jnp.int32) // lines % 2 == 0)[None, :]
    base_a = jnp.where(is_real, cosine, sine).astype(BF16)
    base_b = jnp.where(is_real, -sine, cosine).astype(BF16)

    partial_lines = call(
        forward_kernel, shape((cols, coils * lanes), BF16), [VMEM] * 6, 2 * 10**9, 3 * 10**6
    )(u, phi, coil_maps, base_a, base_b, dft)
    parts = lax.all_to_all(
        partial_lines.reshape(members, span, coils * lanes), "vox", 0, 0, tiled=True
    )
    residual = call(
        residual_kernel, shape((members, span, coils * lanes), BF16), [VMEM] * 2, 10**7, 10**6
    )(parts, kspace_data.reshape(frames, coils, 2 * lines, span))
    residual = lax.all_to_all(residual, "vox", 0, 0, tiled=True)
    residual = residual.reshape(cols, coils * lanes)

    z_high = lax.axis_index("frm") // owners
    size = cols // 2 // owners * frames * 2 * rows // (4 * rows)

    def backward(offset, with_phi):
        depth = size + (frames if with_phi else 0)
        return call(
            lambda *refs: backward_kernel(with_phi, *refs),
            (shape((owners, depth, 4 * rows), BF16), shape((frames, rank), F32)),
            [SMEM] + [VMEM] * 7,
            2 * 10**9,
            3 * 10**6,
        )(offset.reshape(1), residual, u, phi, coil_maps, base_a, base_b, dft)

    groups = [list(range(owners)), list(range(owners, devices))]

    def exchange(chunks):
        return lax.all_to_all(chunks, "frm", 0, 0, tiled=True, axis_index_groups=groups)

    far_chunks, far_basis = backward((1 - z_high) * (cols // 2), True)
    far_chunks = exchange(far_chunks)
    near_chunks, near_basis = backward(z_high * (cols // 2), False)
    near_chunks = exchange(near_chunks)
    basis_term = far_basis + near_basis
    basis_all = lax.all_to_all(
        jnp.broadcast_to(basis_term[None], (members, frames, rank)), "vox", 0, 0, tiled=True
    )
    far = call(far_kernel, shape((2 * rank, 4 * rows), BF16), [VMEM], 10**7, 10**6)(far_chunks)
    far = lax.ppermute(far, "frm", [(i, (i + owners) % devices) for i in range(devices)])
    coeff_grad = call(
        near_kernel,
        shape((cols // devices, 2, rank, rows), F32),
        [VMEM] * 3,
        10**7,
        10**6,
    )(near_chunks, far_chunks, far)
    basis_grad = (jnp.sum(basis_all, axis=0) / height).T
    return (coeff_grad, basis_grad)


def solution(mesh):
    placed = (
        P(None, None, "vox", None),
        P(None, "frm"),
        P(None, None, "vox", None),
        P("frm", None),
        P("frm", None, None, None, "vox"),
    )
    return jax.shard_map(
        local,
        mesh=mesh,
        in_specs=placed,
        out_specs=(P("frm", None, None, "vox"), P(None, "frm")),
        check_vma=False,
    )
```

time: 805 us -> 115 us (0.14)
  the two profiles are of different devices: /device:TPU:31 before, /device:TPU:2 now
where the time goes in v1:
time: 115 us; the launch traced here: 114 us
  blocking collectives  44.4 us (39%)
  waiting for transfers between devices  27.6 us (24%)
  starting transfers between devices  26 us (23%)
  Pallas kernels  8.3 us (7%)
  local copies, waits for them, and re-layouts  5.31 us (5%)
  other arithmetic  1.45 us (1%)
    all_to_all x1, blocking collectives, local(): lax.all_to_all(partial_lines.reshape(members, span, coils * lanes), 'vox'...  29.1 us
    all_to_all x1, waiting for transfers between devices, local(): residual = lax.all_to_all(residual, 'vox', 0, 0, tiled=True)  16.3 us
    all_to_all x1, blocking collectives, local(): lax.all_to_all(jnp.broadcast_to(basis_term[None], (members, frames, rank)...  15.3 us
    all_to_all x2, starting transfers between devices, exchange(): lax.all_to_all(chunks, 'frm', 0, 0, tiled=True, axis_index_groups=groups)  12.6 us
    ppermute x1, starting transfers between devices, local(): lax.ppermute(far, 'frm', [(i, (i + owners) % devices) for i in range(devi...  8.21 us
    all_to_all x2, waiting for transfers between devices, exchange(): lax.all_to_all(chunks, 'frm', 0, 0, tiled=True, axis_index_groups=groups)  5.78 us
    ppermute x1, waiting for transfers between devices, local(): lax.ppermute(far, 'frm', [(i, (i + owners) % devices) for i in range(devi...  5.53 us
    all_to_all x1, starting transfers between devices, local(): residual = lax.all_to_all(residual, 'vox', 0, 0, tiled=True)  5.2 us
  transfers between devices with their start and end apart: 4, of which 3 were waited for; matrix products, arithmetic and copies ran while one was open for 2% of the time, Pallas kernels for 0%

profile of v1, /device:TPU:2, one launch (start us, length us, event | category | flops | bytes accessed | tf_op | source)
XLA Modules:
  0.0 113.9 jit_solution(12839421133537303255)
XLA Ops:
  0.6 0.0 copy-start.8
  0.7 0.7 copy-done.8
  1.3 0.1 mul.37
  1.4 0.2 select_convert_fusion
  1.6 0.0 copy-start.5
  1.6 0.7 copy-done.5
  2.3 0.0 copy-start.1
  2.3 1.2 %copy-done.1 = bf16[2,32,32,256]{3,2,1,0:T(8,128)(2,1)S(1)} copy-done((bf16[2,32,32,256]{3,2,1,0:T(8,128)(2,1)S(1)}, bf16[2,32,32,256]{3,2,1,0:T(8,128)(2,1)}, u32[]{:S(2)}) %copy-start.1) | copy-done | bytes 1048600
  3.5 0.0 copy-start.3
  3.5 0.9 copy-done.3
  4.4 0.0 copy-start.6
  4.4 1.0 copy-done.6
  5.5 0.0 copy-start.7
  5.5 2.3 %shard_map.77 = bf16[256,512]{1,0:T(8,128)(2,1)S(1)} custom-call(bf16[2,1024,256]{2,1,0:T(8,128)(2,1)S(1)} %bitcast.13, bf16[8,32]{1,0:T(8,128)(2,1)S(1)} %bitcast.16, bf16[2,4,32,256]{3,2,1,0:T(8,128)(2,1)S(1)} %copy-done.3, bf16[32,128]{1,0:T(8,128)(2,1)S(1)} %get-tuple-element.11.base_a_ref.refs_5_, ...), custom_call_target="tpu_custom_call" | custom-call | flops 2000000000 | bytes 3000000 | tf_op jit(solution)/shard_map/pallas_call | solution.py:262
  7.7 0.0 copy-start
  7.7 0.0 copy-start.2
  7.8 29.1 %all_to_all.25.parts_ref = bf16[8,32,512]{2,1,0:T(8,128)(2,1)S(1)} all-to-all(bf16[8,32,512]{2,1,0:T(8,128)(2,1)S(1)} %bitcast.11), channel_id=1, replica_groups=mesh['vox'=8,'frm'=64] {'vox'}, dimensions={0} | all-to-all | bytes 524288 | tf_op jit(solution)/shard_map/all_to_all | solution.py:265
  36.9 0.0 copy-done
  36.9 0.9 shard_map.78
  37.8 0.0 copy-start.4
  37.8 5.2 %all-to-all-start.1 = ((bf16[8,32,512]{2,1,0:T(8,128)(2,1)}), bf16[8,32,512]{2,1,0:T(8,128)(2,1)S(1)}, u32[]{:S(2)}, u32[]{:S(2)}) async-start(bf16[8,32,512]{2,1,0:T(8,128)(2,1)} %shard_map.78), calls=%async_computation.1 | async-start | bytes 524288 | tf_op jit(solution)/shard_map/all_to_all | solution.py:271
  43.0 16.3 %all-to-all-done.1 = bf16[8,32,512]{2,1,0:T(8,128)(2,1)S(1)} async-done(((bf16[8,32,512]{2,1,0:T(8,128)(2,1)}), bf16[8,32,512]{2,1,0:T(8,128)(2,1)S(1)}, u32[]{:S(2)}, u32[]{:S(2)}) %all-to-all-start.1) | async-done | bytes 262176 | tf_op jit(solution)/shard_map/all_to_all | solution.py:271
  59.3 0.0 copy-done.7
  59.3 0.0 copy-done.2
  59.3 0.0 copy-done.4
  59.3 1.9 %shard_map.80 = (bf16[32,24,128]{2,1,0:T(8,128)(2,1)}, f32[8,32]{1,0:T(8,128)S(1)}) custom-call(s32[1]{0:T(128)} %bitcast.6.refs_0_, bf16[256,512]{1,0:T(8,128)(2,1)S(1)} %bitcast.9, bf16[2,1024,256]{2,1,0:T(8,128)(2,1)S(1)} %bitcast.14, bf16[8,32]{1,0:T(8,128)(2,1)S(1)} %bitcast.17, bf16[2,4,32,256]{3,2,1,0:T(8,128)(2,1)S(1)} %copy-done.4, ...), custom_call_target="tpu_custom_call" | custom-call | flops 2000000000 | bytes 3000000 | tf_op jit(solution)/shard_map/pallas_call | solution.py:279
  61.2 1.9 %shard_map.79 = (bf16[32,16,128]{2,1,0:T(8,128)(2,1)}, f32[8,32]{1,0:T(8,128)S(1)}) custom-call(s32[1]{0:T(128)} %bitcast.refs_0_, bf16[256,512]{1,0:T(8,128)(2,1)S(1)} %bitcast.10, bf16[2,1024,256]{2,1,0:T(8,128)(2,1)S(1)} %bitcast.15, bf16[8,32]{1,0:T(8,128)(2,1)S(1)} %bitcast.18, bf16[2,4,32,256]{3,2,1,0:T(8,128)(2,1)S(1)} %copy-done.4, ...), custom_call_target="tpu_custom_call" | custom-call | flops 2000000000 | bytes 3000000 | tf_op jit(solution)/shard_map/pallas_call | solution.py:279
  63.0 0.1 reshape.61
  63.1 15.3 %all_to_all.26 = f32[8,1,256]{2,1,0:T(1,128)S(1)} all-to-all(f32[8,1,256]{2,1,0:T(1,128)S(1)} %reshape.61), channel_id=1, replica_groups=mesh['vox'=8,'frm'=64] {'vox'}, dimensions={0} | all-to-all | bytes 16384 | tf_op jit(solution)/shard_map/all_to_all | solution.py:297
  78.4 7.6 %all-to-all-start.3 = ((bf16[32,24,128]{2,1,0:T(8,128)(2,1)}), bf16[32,24,128]{2,1,0:T(8,128)(2,1)S(1)}, u32[]{:S(2)}, u32[]{:S(2)}) async-start(bf16[32,24,128]{2,1,0:T(8,128)(2,1)} %get-tuple-element.7), calls=%async_computation.3 | async-start | bytes 393216 | tf_op jit(solution)/shard_map/all_to_all | solution.py:290
  86.1 0.5 broadcast.89
  86.6 0.7 reduce
  87.3 0.1 reshape.62
  87.3 5.8 %all-to-all-done.3.a_ref = bf16[32,24,128]{2,1,0:T(8,128)(2,1)S(1)} async-done(((bf16[32,24,128]{2,1,0:T(8,128)(2,1)}), bf16[32,24,128]{2,1,0:T(8,128)(2,1)S(1)}, u32[]{:S(2)}, u32[]{:S(2)}) %all-to-all-start.3) | async-done | bytes 196640 | tf_op jit(solution)/shard_map/all_to_all | solution.py:290
  93.1 5.0 %all-to-all-start.2 = ((bf16[32,16,128]{2,1,0:T(8,128)(2,1)}), bf16[32,16,128]{2,1,0:T(8,128)(2,1)S(1)}, u32[]{:S(2)}, u32[]{:S(2)}) async-start(bf16[32,16,128]{2,1,0:T(8,128)(2,1)} %get-tuple-element.6), calls=%async_computation.2 | async-start | bytes 262144 | tf_op jit(solution)/shard_map/all_to_all | solution.py:290
  98.1 0.3 shard_map.81
  98.5 8.2 %collective-permute-start = (bf16[64,128]{1,0:T(8,128)(2,1)S(1)}, bf16[64,128]{1,0:T(8,128)(2,1)S(1)}, u32[]{:S(2)}, u32[]{:S(2)}) collective-permute-start(bf16[64,128]{1,0:T(8,128)(2,1)S(1)} %shard_map.81), channel_id=1, source_target_pairs={{0,32},{1,33},{2,34},{3,35},{4,36},{5,37},{6,38},{7,39},{8,40},{9,... | collective-permute-start | bytes 49160 | tf_op jit(solution)/shard_map/ppermute | solution.py:301
  106.7 0.6 multiply_bitcast_fusion
  107.3 0.0 all-to-all-done.2.b_ref
  107.3 5.5 %collective-permute-done.far_ref = bf16[64,128]{1,0:T(8,128)(2,1)S(1)} collective-permute-done((bf16[64,128]{1,0:T(8,128)(2,1)S(1)}, bf16[64,128]{1,0:T(8,128)(2,1)S(1)}, u32[]{:S(2)}, u32[]{:S(2)}) %collective-permute-start) | collective-permute-done | bytes 16416 | tf_op jit(solution)/shard_map/ppermute | solution.py:301
  112.8 1.1 shard_map.82
  (6 shorter events, 0.0 us)
Async XLA Ops:
  0.6 0.7 copy-start.8
  1.6 0.7 copy-start.5
  2.3 1.2 %copy-start.1 = (bf16[2,32,32,256]{3,2,1,0:T(8,128)(2,1)S(1)}, bf16[2,32,32,256]{3,2,1,0:T(8,128)(2,1)}, u32[]{:S(2)}) copy-start(bf16[2,32,32,256]{3,2,1,0:T(8,128)(2,1)} %param.6) | copy-start | bytes 3145732
  3.5 0.9 copy-start.3
  4.4 1.0 copy-start.6
  5.5 53.8 %copy-start.7 = (bf16[512,512]{1,0:T(8,128)(2,1)S(1)}, bf16[512,512]{1,0:T(8,128)(2,1)}, u32[]{:S(2)}) copy-start(bf16[512,512]{1,0:T(8,128)(2,1)} %constant.83.clone.dft_ref.refs_7_) | copy-start | bytes 1572868
  7.7 29.2 %copy-start = (bf16[8,4,2,8,32]{4,3,2,1,0:T(8,128)(2,1)S(1)}, bf16[8,4,2,8,32]{4,3,2,1,0:T(8,128)(2,1)}, u32[]{:S(2)}) copy-start(bf16[8,4,2,8,32]{4,3,2,1,0:T(8,128)(2,1)} %param.10) | copy-start | bytes 98308
  7.7 51.5 %copy-start.2 = (bf16[2,32,32,256]{3,2,1,0:T(8,128)(2,1)S(1)}, bf16[2,32,32,256]{3,2,1,0:T(8,128)(2,1)}, u32[]{:S(2)}) copy-start(bf16[2,32,32,256]{3,2,1,0:T(8,128)(2,1)} %param.6) | copy-start | bytes 3145732
  37.8 21.5 %copy-start.4 = (bf16[2,4,32,256]{3,2,1,0:T(8,128)(2,1)S(1)}, bf16[2,4,32,256]{3,2,1,0:T(8,128)(2,1)}, u32[]{:S(2)}) copy-start(bf16[2,4,32,256]{3,2,1,0:T(8,128)(2,1)} %refs_4_.3) | copy-start | bytes 393220
  37.8 21.5 %all-to-all-start.1 = ((bf16[8,32,512]{2,1,0:T(8,128)(2,1)}), bf16[8,32,512]{2,1,0:T(8,128)(2,1)S(1)}, u32[]{:S(2)}, u32[]{:S(2)}) async-start(bf16[8,32,512]{2,1,0:T(8,128)(2,1)} %shard_map.78), calls=%async_computation.1 | async-start | bytes 524288 | tf_op jit(solution)/shard_map/all_to_all | solution.py:271
  78.4 14.7 %all-to-all-start.3 = ((bf16[32,24,128]{2,1,0:T(8,128)(2,1)}), bf16[32,24,128]{2,1,0:T(8,128)(2,1)S(1)}, u32[]{:S(2)}, u32[]{:S(2)}) async-start(bf16[32,24,128]{2,1,0:T(8,128)(2,1)} %get-tuple-element.7), calls=%async_computation.3 | async-start | bytes 393216 | tf_op jit(solution)/shard_map/all_to_all | solution.py:290
  93.1 14.2 %all-to-all-start.2 = ((bf16[32,16,128]{2,1,0:T(8,128)(2,1)}), bf16[32,16,128]{2,1,0:T(8,128)(2,1)S(1)}, u32[]{:S(2)}, u32[]{:S(2)}) async-start(bf16[32,16,128]{2,1,0:T(8,128)(2,1)} %get-tuple-element.6), calls=%async_computation.2 | async-start | bytes 262144 | tf_op jit(solution)/shard_map/all_to_all | solution.py:290
  98.5 14.3 %collective-permute-start = (bf16[64,128]{1,0:T(8,128)(2,1)S(1)}, bf16[64,128]{1,0:T(8,128)(2,1)S(1)}, u32[]{:S(2)}, u32[]{:S(2)}) collective-permute-start(bf16[64,128]{1,0:T(8,128)(2,1)S(1)} %shard_map.81), channel_id=1, source_target_pairs={{0,32},{1,33},{2,34},{3,35},{4,36},{5,37},{6,38},{7,39},{8,40},{9,... | collective-permute-start | bytes 49160 | tf_op jit(solution)/shard_map/ppermute | solution.py:301

commit v2 on v1

v2 whole, which is shorter than its diff:
```python
import functools
import math

import jax
import jax.numpy as jnp
import numpy as np
from jax import lax
from jax.experimental import pallas as pl
from jax.experimental.pallas import tpu as pltpu
from jax.sharding import PartitionSpec as P

F32 = jnp.float32
BF16 = jnp.bfloat16
VMEM = pl.BlockSpec(memory_space=pltpu.VMEM)
SMEM = pl.BlockSpec(memory_space=pltpu.SMEM)
HBM = pl.BlockSpec(memory_space=pltpu.HBM)


def dot_nn(a, b):
    return lax.dot_general(a, b, (((1,), (0,)), ((), ())), preferred_element_type=F32)


def dot_nt(a, b, precision=None):
    return lax.dot_general(
        a, b, (((1,), (1,)), ((), ())), preferred_element_type=F32, precision=precision
    )


def dot_tn(a, b, precision=None):
    return lax.dot_general(
        a, b, (((0,), (0,)), ((), ())), preferred_element_type=F32, precision=precision
    )


def iota(shape, axis):
    return lax.broadcasted_iota(jnp.int32, shape, axis)


def one_hot(condition):
    return jnp.where(condition, 1.0, 0.0).astype(BF16)


def dft_block(length):
    indices = np.arange(length, dtype=np.int64)
    phases = (indices[:, None] * indices[None, :]) % length
    angles = phases.astype(np.float32) * np.float32(2.0 * math.pi / length)
    factor = np.float32(1.0 / math.sqrt(length))
    cosine = np.cos(angles) * factor
    sine = -np.sin(angles) * factor
    top = np.concatenate([cosine, -sine], axis=1)
    low = np.concatenate([sine, cosine], axis=1)
    return np.concatenate([top, low], axis=0).astype(BF16)


def line_blocks(base, frames):
    lane_frame = iota(base.shape, 1) // (base.shape[1] // frames)
    wide = base.astype(F32)
    return jnp.concatenate(
        [jnp.where(lane_frame == t, wide, 0.0).astype(BF16) for t in range(frames)], axis=0
    )


def over_frames(block, frames):
    return jnp.concatenate([block] * frames, axis=0)


def line_tables(v, lines_ref, dft_ref, rows, frames):
    cols = dft_ref.shape[0] // 2
    count = lines_ref.shape[1]
    lanes = frames * 2 * count
    spread = one_hot(iota((count, lanes), 1) % count == iota((count, lanes), 0))
    wide = dot_nn(lines_ref[...].astype(F32).astype(BF16), spread)
    mine = iota((frames, lanes), 1) // (2 * count) == iota((frames, lanes), 0)
    number = jnp.sum(jnp.where(mine, wide, 0.0), axis=0, keepdims=True).astype(jnp.int32)
    chosen = one_hot(iota((cols, lanes), 0) == number)
    first = pl.multiple_of(v * rows, rows)
    cosine = dot_nn(dft_ref[pl.ds(first, rows), :cols], chosen)
    sine = dot_nn(dft_ref[pl.ds(pl.multiple_of(cols + first, rows), rows), :cols], chosen)
    is_real = iota((rows, lanes), 1) // count % 2 == 0
    return jnp.where(is_real, cosine, sine), jnp.where(is_real, -sine, cosine)


def basis_tile(phi_ref):
    rank, frames = phi_ref.shape[1], phi_ref.shape[0]
    quads = frames // 2
    lanes = 4 * rank
    row, lane = iota((frames, lanes), 0), iota((frames, lanes), 1)
    spread = one_hot(iota((rank, lanes), 1) % rank == iota((rank, lanes), 0))
    phi_wide = dot_nn(phi_ref[...], spread).astype(BF16)
    square = (frames, frames)
    first = dot_nn(one_hot(iota(square, 1) == iota(square, 0) % quads * 2), phi_wide)
    second = dot_nn(one_hot(iota(square, 1) == iota(square, 0) % quads * 2 + 1), phi_wide)
    tile = jnp.where(lane // rank % 2 == 0, first, second)
    return jnp.where(lane // (2 * rank) == row // quads, tile, 0.0)


def forward_kernel(
    v_ref, u_hbm, phi_hbm, maps_hbm, lines_hbm, dft_hbm, out_ref, tables_ref,
    u_ref, phi_ref, maps_ref, lines_ref, dft_ref, sems,
):
    copies = [
        pltpu.make_async_copy(source, target, sems.at[i])
        for i, (source, target) in enumerate(
            [
                (phi_hbm, phi_ref),
                (lines_hbm, lines_ref),
                (dft_hbm, dft_ref),
                (u_hbm, u_ref),
                (maps_hbm, maps_ref),
            ]
        )
    ]
    for copy in copies:
        copy.start()
    rank, frames = phi_ref.shape[1], phi_ref.shape[0]
    coils, rows, cols = maps_ref.shape[1:]
    spread = one_hot(iota((rank, rank * rows), 1) // rows == iota((rank, rank * rows), 0))
    same_row = iota((rows, rank * rows), 1) % rows == iota((rows, rank * rows), 0)
    copies[0].wait()
    phi_wide = dot_nn(phi_ref[...], spread)
    mix = jnp.concatenate(
        [
            jnp.where(same_row, jnp.broadcast_to(phi_wide[t : t + 1], same_row.shape), 0.0).astype(BF16)
            for t in range(frames)
        ],
        axis=0,
    )
    copies[1].wait()
    copies[2].wait()
    base_a, base_b = line_tables(v_ref[0], lines_ref, dft_ref, rows, frames)
    lines = base_a.shape[1]
    tables = [base_a, base_b, basis_tile(phi_ref)]
    tables.append(jnp.zeros((tables_ref.shape[0] - sum(t.shape[0] for t in tables), lines), F32))
    tables_ref[...] = jnp.concatenate(tables, axis=0).astype(BF16)
    sampling = jnp.concatenate(
        [line_blocks(base_a.astype(BF16), frames), line_blocks(base_b.astype(BF16), frames)], axis=0
    )
    quad, span = out_ref.shape[0], out_ref.shape[1] // 2
    copies[3].wait()
    copies[4].wait()
    img_real = dot_nn(mix, u_ref[0])
    img_imag = dot_nn(mix, u_ref[1])
    for c in range(coils):
        map_real = over_frames(maps_ref[0, c].astype(F32), frames)
        map_imag = over_frames(maps_ref[1, c].astype(F32), frames)
        coil_real = (map_real * img_real - map_imag * img_imag).astype(BF16)
        coil_imag = (map_real * img_imag + map_imag * img_real).astype(BF16)
        coil = jnp.concatenate([coil_real, coil_imag], axis=1)
        hybrid = dot_nt(dft_ref[...], coil).astype(BF16)
        hybrid = jnp.concatenate([hybrid[:cols], hybrid[cols:]], axis=1)
        found = dot_nn(hybrid, sampling).astype(BF16)
        for b in range(2 * quad):
            out_ref[b % quad, b // quad * span : (b // quad + 1) * span, c * lines : (c + 1) * lines] = (
                found[b * span : (b + 1) * span]
            )


def quad_kernel(half_ref, parts_ref, data_ref, out_ref):
    total = parts_ref[0].astype(F32)
    for m in range(1, parts_ref.shape[0]):
        total = total + parts_ref[m].astype(F32)
    frames, coils, _, span = data_ref.shape
    data = jnp.concatenate(
        [data_ref[t, c] for c in range(coils) for t in range(frames)], axis=0
    )
    eye = one_hot(iota((span, span), 0) == iota((span, span), 1))
    measured = dot_nt(eye, data)
    for h in range(2):
        rows = slice(h * span, (h + 1) * span)
        out_ref[rows, :] = (total[rows] - jnp.where(half_ref[0] == h, measured, 0.0)).astype(BF16)


def residual_kernel(mine_ref, other_ref, out_ref):
    residual = (mine_ref[...].astype(F32) + other_ref[...].astype(F32)).astype(BF16)
    for m in range(out_ref.shape[0]):
        out_ref[m] = residual


def backward_kernel(
    res_ref, u_ref, maps_ref, tables_ref, dft_ref, out_ref, basis_ref
):
    coils, rows, cols = maps_ref.shape[1:]
    frames, rank = basis_ref.shape[0], u_ref.shape[1] // rows
    lines = tables_ref.shape[1]
    quad, span = res_ref.shape[0], res_ref.shape[1] // 2
    points = frames * rows
    sampling = jnp.concatenate(
        [line_blocks(tables_ref[i * rows : (i + 1) * rows, :], frames) for i in range(2)], axis=0
    )
    grad_real = jnp.zeros((points, cols), F32)
    grad_imag = jnp.zeros((points, cols), F32)
    for c in range(coils):
        found = jnp.concatenate(
            [
                res_ref[b % quad, b // quad * span : (b // quad + 1) * span, c * lines : (c + 1) * lines]
                for b in range(2 * quad)
            ],
            axis=0,
        )
        back = dot_nt(sampling, found).astype(BF16)
        back = jnp.concatenate([back[:points], back[points:]], axis=1)
        adj = dot_nn(back, dft_ref[...])
        adj_real, adj_imag = adj[:, :cols], adj[:, cols:]
        map_real = over_frames(maps_ref[0, c].astype(F32), frames)
        map_imag = over_frames(maps_ref[1, c].astype(F32), frames)
        grad_real = grad_real + (map_real * adj_real + map_imag * adj_imag)
        grad_imag = grad_imag + (map_real * adj_imag - map_imag * adj_real)
    grad_real = grad_real.astype(BF16)
    grad_imag = grad_imag.astype(BF16)
    half = cols // 2
    quads = frames // 2
    places = half * quads
    owners = out_ref.shape[0]
    size = places // owners
    for z in range(2):
        moved = jnp.zeros((places, 4 * rows), F32)
        for q in range(quads):
            piece = jnp.concatenate(
                [
                    g[q * 2 * rows : (q + 1) * 2 * rows, z * half : (z + 1) * half]
                    for g in (grad_real, grad_imag)
                ],
                axis=0,
            )
            chosen = one_hot(iota((places, half), 0) == iota((places, half), 1) * quads + q)
            moved = moved + dot_nt(chosen, piece)
        out_ref[:, z * size : (z + 1) * size, :] = moved.astype(BF16).reshape(
            owners, size, 4 * rows
        )
    tile = tables_ref[2 * rows : 2 * rows + frames, :]
    for d in range(owners):
        out_ref[d, 2 * size :, :] = tile
    both = jnp.concatenate([grad_real, grad_imag], axis=1)
    coeffs = jnp.concatenate([u_ref[0], u_ref[1]], axis=1)
    cross = dot_nt(coeffs, both).reshape(rank, rows, points)
    keep = iota((rows, points), 1) % rows == iota((rows, points), 0)
    per_rank = jnp.concatenate(
        [
            jnp.sum(jnp.where(keep, cross[l], 0.0), axis=0, keepdims=True)
            for l in range(rank)
        ],
        axis=0,
    )
    frame_sum = jnp.where(
        iota((frames, points), 1) // rows == iota((frames, points), 0), 1.0, 0.0
    )
    per_rank = jnp.concatenate(
        [per_rank, jnp.zeros((basis_ref.shape[1] - rank, points), F32)], axis=0
    )
    basis_ref[...] = dot_nt(frame_sum, per_rank, lax.Precision.HIGHEST)


def tiles(ref, first):
    owners, lanes = ref.shape[0], ref.shape[2]
    wide = ref[:, pl.ds(first, 8), :].astype(F32)
    return wide.reshape(owners * 8, lanes).astype(BF16)


def combine(ref, first, rank):
    weights = tiles(ref, 32)
    summed = []
    for h in range(2):
        product = dot_tn(weights, tiles(ref, pl.multiple_of(first + 8 * h, 8)))
        halves = []
        for x in range(2):
            even = product[(2 * x) * rank : (2 * x + 1) * rank]
            odd = product[(2 * x + 1) * rank : (2 * x + 2) * rank]
            halves.append(even + pltpu.roll(odd, odd.shape[1] - rank, 1))
        summed.append(jnp.concatenate(halves, axis=0))
    lane = iota(summed[0].shape, 1)
    return jnp.where(lane // rank % 2 == 0, summed[0], pltpu.roll(summed[1], rank, 1))


def contract_kernel(z_ref, chunks_ref, far_ref, near_ref):
    rank = far_ref.shape[0] // 2
    z = z_ref[0]
    far_ref[...] = combine(chunks_ref, (1 - z) * 16, rank).astype(BF16)
    near_ref[...] = combine(chunks_ref, z * 16, rank)


def sum_kernel(*refs):
    total = refs[0][...]
    for ref in refs[1:-1]:
        total = total + ref[...]
    out_ref = refs[-1]
    if len(out_ref.shape) == len(total.shape):
        out_ref[...] = total
    else:
        for m in range(out_ref.shape[0]):
            out_ref[m] = total


def finish_kernel(height, near_ref, far_ref, basis_ref, out_ref, basis_out_ref):
    rank, rows = out_ref.shape[2:]
    total = near_ref[...] + far_ref[...].astype(F32)
    for h in range(2):
        for x in range(2):
            for p in range(2):
                lane = p * 2 * rows + h * rows
                out_ref[h * 2 + x, p] = total[x * rank : (x + 1) * rank, lane : lane + rows]
    basis = sum(basis_ref[m] for m in range(basis_ref.shape[0])) / height
    basis_out_ref[...] = basis[:, :rank]


def call(kernel, out_shape, specs, flops, bytes_accessed, scratch=(), vmem_mib=40):
    return pl.pallas_call(
        kernel,
        out_shape=out_shape,
        in_specs=specs,
        out_specs=jax.tree.map(lambda _: VMEM, out_shape),
        scratch_shapes=scratch,
        compiler_params=pltpu.CompilerParams(vmem_limit_bytes=vmem_mib * 2**20),
        cost_estimate=pl.CostEstimate(
            flops=flops, bytes_accessed=bytes_accessed, transcendentals=0
        ),
    )


def shape(dims, dtype):
    return jax.ShapeDtypeStruct(dims, dtype)


def swapped(count, step):
    return [(i, i ^ step) for i in range(count)]


def steps(spatial_coeffs, temporal_basis, coil_maps, line_index, kspace_data):
    rank, rows, cols = spatial_coeffs.shape[1:]
    frames = temporal_basis.shape[1]
    coils = coil_maps.shape[1]
    lines = line_index.shape[1]
    members = lax.axis_size("vox")
    devices = lax.axis_size("frm")
    owners = devices // 2
    span = kspace_data.shape[4]
    quad = members // 2
    quads = [list(range(quad)), list(range(quad, members))]
    height = rows * members
    lanes = frames * 2 * lines

    dft = jnp.asarray(dft_block(cols))
    u = spatial_coeffs.reshape(2, rank * rows, cols)
    phi = temporal_basis.T
    partial_lines, tables = call(
        forward_kernel,
        (shape((quad, 2 * span, coils * lanes), BF16), shape((2 * rows + 16, lanes), BF16)),
        [SMEM] + [HBM] * 5,
        2 * 10**9,
        3 * 10**6,
        scratch=[
            pltpu.VMEM(u.shape, BF16),
            pltpu.VMEM(phi.shape, BF16),
            pltpu.VMEM(coil_maps.shape, BF16),
            pltpu.VMEM(line_index.shape, jnp.int32),
            pltpu.VMEM(dft.shape, BF16),
            pltpu.SemaphoreType.DMA((5,)),
        ],
        vmem_mib=63,
    )(lax.axis_index("vox").reshape(1), u, phi, coil_maps, line_index, dft)
    parts = lax.all_to_all(partial_lines, "vox", 0, 0, tiled=True, axis_index_groups=quads)
    block = (2 * span, coils * lanes)
    mine = call(quad_kernel, shape(block, BF16), [SMEM] + [VMEM] * 2, 10**7, 10**6)(
        (lax.axis_index("vox") // quad).reshape(1),
        parts,
        kspace_data.reshape(frames, coils, 2 * lines, span),
    )
    other = lax.ppermute(mine, "vox", swapped(members, quad))
    residual = call(residual_kernel, shape((quad, *block), BF16), [VMEM] * 2, 10**7, 10**6)(
        mine, other
    )
    residual = lax.all_to_all(residual, "vox", 0, 0, tiled=True, axis_index_groups=quads)

    z_high = lax.axis_index("frm") // owners
    depth = cols // devices * 2 * frames // 2 + frames
    chunks, basis_term = call(
        backward_kernel,
        (shape((owners, depth, 4 * rows), BF16), shape((frames, lanes), F32)),
        [VMEM] * 5,
        4 * 10**9,
        3 * 10**6,
    )(residual, u, coil_maps, tables, dft)
    groups = [list(range(owners)), list(range(owners, devices))]
    chunks = lax.all_to_all(chunks, "frm", 0, 0, tiled=True, axis_index_groups=groups)
    basis_part = lax.ppermute(basis_term, "vox", swapped(members, quad))
    basis_term = call(
        sum_kernel, shape((quad, frames, lanes), F32), [VMEM] * 2, 10**4, 10**4
    )(basis_term, basis_part)
    far, near = call(
        contract_kernel,
        (shape((2 * rank, 4 * rows), BF16), shape((2 * rank, 4 * rows), F32)),
        [SMEM, VMEM],
        10**7,
        10**6,
    )(z_high.reshape(1), chunks)
    far = lax.ppermute(far, "frm", swapped(devices, owners))
    basis_all = lax.all_to_all(
        basis_term, "vox", 0, 0, tiled=True,
        axis_index_groups=quads,
    )
    coeff_grad, basis_grad = call(
        functools.partial(finish_kernel, height),
        (shape((cols // devices, 2, rank, rows), F32), shape((frames, rank), F32)),
        [VMEM] * 3,
        10**6,
        10**6,
    )(near, far, basis_all)
    return (coeff_grad, basis_grad.T)


def solution(mesh):
    placed = (
        P(None, None, "vox", None),
        P(None, "frm"),
        P(None, None, "vox", None),
        P("frm", None),
        P("frm", None, None, None, "vox"),
    )
    return jax.shard_map(
        steps,
        mesh=mesh,
        in_specs=placed,
        out_specs=(P("frm", None, None, "vox"), P(None, "frm")),
        check_vma=False,
    )
```

time: 115 us -> 84.1 us (0.73)
  the two profiles are of different devices: /device:TPU:2 before, /device:TPU:34 now
where the time goes in v2:
time: 84.1 us; the launch traced here: 83.6 us
  starting transfers between devices  46.9 us (56%)
  waiting for transfers between devices  16.2 us (19%)
  blocking collectives  10.8 us (13%)
  Pallas kernels  8.97 us (11%)
    ppermute x1, starting transfers between devices, steps(): far = lax.ppermute(far, 'frm', swapped(devices, owners))  10.9 us
    all_to_all x1, blocking collectives, steps(): lax.all_to_all(residual, 'vox', 0, 0, tiled=True, axis_index_groups=quads)  10.8 us
    ppermute x1, starting transfers between devices, steps(): other = lax.ppermute(mine, 'vox', swapped(members, quad))  9.23 us
    ppermute x1, starting transfers between devices, steps(): basis_part = lax.ppermute(basis_term, 'vox', swapped(members, quad))  8.02 us
    all_to_all x1, starting transfers between devices, steps(): lax.all_to_all(chunks, 'frm', 0, 0, tiled=True, axis_index_groups=groups)  7.62 us
    all_to_all x1, waiting for transfers between devices, steps(): lax.all_to_all(partial_lines, 'vox', 0, 0, tiled=True, axis_index_groups=...  7.05 us
    all_to_all x1, starting transfers between devices, steps(): lax.all_to_all(partial_lines, 'vox', 0, 0, tiled=True, axis_index_groups=...  6.15 us
    all_to_all x1, starting transfers between devices, steps(): lax.all_to_all(basis_term, 'vox', 0, 0, tiled=True, axis_index_groups=quads)  5 us
  transfers between devices with their start and end apart: 6, of which 4 were waited for; matrix products, arithmetic and copies ran while one was open for 0% of the time, Pallas kernels for 1%

profile of v2, /device:TPU:34, one launch (start us, length us, event | category | flops | bytes accessed | tf_op | source)
XLA Modules:
  0.0 83.6 jit_solution(16746829772262231008)
XLA Ops:
  0.6 4.3 %shard_map.77 = (bf16[4,64,512]{2,1,0:T(8,128)(2,1)}, bf16[80,128]{1,0:T(8,128)(2,1)}) custom-call(s32[1]{0:T(128)} %bitcast.2.v_ref, bf16[2,1024,256]{2,1,0:T(8,128)(2,1)} %bitcast.8, bf16[8,32]{1,0:T(8,128)(2,1)} %bitcast.11, bf16[2,4,32,256]{3,2,1,0:T(8,128)(2,1)} %maps_ref.1, s32[8,8]{1,0:T(8,128)} %lines_hbm.1, ...), custom_call_target="tpu_custom_call" | custom-call | flops 2000000000 | bytes 3000000 | tf_op jit(solution)/shard_map/pallas_call | solution.py:344
  5.0 0.0 copy-start
  5.0 0.0 copy-start.1
  5.0 6.1 %all-to-all-start = ((bf16[4,64,512]{2,1,0:T(8,128)(2,1)}), bf16[4,64,512]{2,1,0:T(8,128)(2,1)S(1)}, u32[]{:S(2)}, u32[]{:S(2)}) async-start(bf16[4,64,512]{2,1,0:T(8,128)(2,1)} %get-tuple-element.10), calls=%async_computation | async-start | bytes 524288 | tf_op jit(solution)/shard_map/all_to_all | solution.py:360
  11.2 7.0 %all-to-all-done.parts_ref = bf16[4,64,512]{2,1,0:T(8,128)(2,1)S(1)} async-done(((bf16[4,64,512]{2,1,0:T(8,128)(2,1)}), bf16[4,64,512]{2,1,0:T(8,128)(2,1)S(1)}, u32[]{:S(2)}, u32[]{:S(2)}) %all-to-all-start) | async-done | bytes 262176 | tf_op jit(solution)/shard_map/all_to_all | solution.py:360
  18.2 0.0 copy-done
  18.2 0.2 shard_map.78.mine_ref
  18.4 0.0 copy-start.3
  18.4 9.2 %collective-permute-start = (bf16[64,512]{1,0:T(8,128)(2,1)S(1)}, bf16[64,512]{1,0:T(8,128)(2,1)S(1)}, u32[]{:S(2)}, u32[]{:S(2)}) collective-permute-start(bf16[64,512]{1,0:T(8,128)(2,1)S(1)} %shard_map.78.mine_ref), channel_id=1, source_target_pairs={{0,256},{64,320},{128,384},{192,448},{256,0},{320,64},{384,128},{4... | collective-permute-start | bytes 196616 | tf_op jit(solution)/shard_map/ppermute | solution.py:367
  27.6 4.1 %collective-permute-done.other_ref = bf16[64,512]{1,0:T(8,128)(2,1)S(1)} collective-permute-done((bf16[64,512]{1,0:T(8,128)(2,1)S(1)}, bf16[64,512]{1,0:T(8,128)(2,1)S(1)}, u32[]{:S(2)}, u32[]{:S(2)}) %collective-permute-start) | collective-permute-done | bytes 65568 | tf_op jit(solution)/shard_map/ppermute | solution.py:367
  31.7 0.0 copy-start.2
  31.8 0.0 copy-start.4
  31.8 10.8 %all_to_all.20.res_ref = bf16[4,64,512]{2,1,0:T(8,128)(2,1)S(1)} all-to-all(bf16[4,64,512]{2,1,0:T(8,128)(2,1)S(1)} %shard_map.79), channel_id=1, replica_groups={{0,64,128,192},{256,320,384,448},{1,65,129,193},{257,321,385,449},{2,66..., dimensions={0} | all-to-all | bytes 524288 | tf_op jit(solution)/shard_map/all_to_all | solution.py:371
  42.6 0.0 copy-done.1
  42.6 0.0 copy-done.3
  42.6 0.0 copy-done.2
  42.6 0.0 copy-done.4
  42.6 2.7 %shard_map.80 = (bf16[32,40,128]{2,1,0:T(8,128)(2,1)}, f32[8,128]{1,0:T(8,128)S(1)}) custom-call(bf16[4,64,512]{2,1,0:T(8,128)(2,1)S(1)} %all_to_all.20.res_ref, bf16[2,1024,256]{2,1,0:T(8,128)(2,1)S(1)} %bitcast.9, bf16[2,4,32,256]{3,2,1,0:T(8,128)(2,1)S(1)} %copy-done.2, bf16[80,128]{1,0:T(8,128)(2,1)S(1)} %copy-done.4, bf16[512,512]{1,0:T(8,128)(2,1)S(1)} %copy-done.3), custom_call_target="tpu_custom_call" | custom-call | flops 4000000000 | bytes 3000000 | tf_op jit(solution)/shard_map/pallas_call | solution.py:375
  45.3 7.6 %all-to-all-start.2 = ((bf16[32,40,128]{2,1,0:T(8,128)(2,1)}), bf16[32,40,128]{2,1,0:T(8,128)(2,1)S(1)}, u32[]{:S(2)}, u32[]{:S(2)}) async-start(bf16[32,40,128]{2,1,0:T(8,128)(2,1)} %get-tuple-element.12), calls=%async_computation.2 | async-start | bytes 655360 | tf_op jit(solution)/shard_map/all_to_all | solution.py:383
  52.9 8.0 %collective-permute-start.2 = (f32[8,128]{1,0:T(8,128)S(1)}, f32[8,128]{1,0:T(8,128)S(1)}, u32[]{:S(2)}, u32[]{:S(2)}) collective-permute-start(f32[8,128]{1,0:T(8,128)S(1)} %get-tuple-element.15.refs_0_), channel_id=1, source_target_pairs={{0,256},{64,320},{128,384},{192,448},{256,0},{320,64},{384,128},{4... | collective-permute-start | bytes 12296 | tf_op jit(solution)/shard_map/ppermute | solution.py:384
  60.9 1.6 %collective-permute-done.2.refs_1_ = f32[8,128]{1,0:T(8,128)S(1)} collective-permute-done((f32[8,128]{1,0:T(8,128)S(1)}, f32[8,128]{1,0:T(8,128)S(1)}, u32[]{:S(2)}, u32[]{:S(2)}) %collective-permute-start.2) | collective-permute-done | bytes 4128 | tf_op jit(solution)/shard_map/ppermute | solution.py:384
  62.5 0.6 shard_map.82
  63.1 0.0 all-to-all-done.2.chunks_ref
  63.1 5.0 %all-to-all-start.3 = ((f32[4,8,128]{2,1,0:T(8,128)}), f32[4,8,128]{2,1,0:T(8,128)S(1)}, u32[]{:S(2)}, u32[]{:S(2)}) async-start(f32[4,8,128]{2,1,0:T(8,128)} %shard_map.82), calls=%async_computation.3 | async-start | bytes 32768 | tf_op jit(solution)/shard_map/all_to_all | solution.py:396
  68.1 0.4 shard_map.81
  68.5 10.9 %collective-permute-start.1 = (bf16[64,128]{1,0:T(8,128)(2,1)S(1)}, bf16[64,128]{1,0:T(8,128)(2,1)S(1)}, u32[]{:S(2)}, u32[]{:S(2)}) collective-permute-start(bf16[64,128]{1,0:T(8,128)(2,1)S(1)} %get-tuple-element.14), channel_id=1, source_target_pairs={{0,32},{1,33},{2,34},{3,35},{4,36},{5,37},{6,38},{7,39},{8,40},{9,... | collective-permute-start | bytes 49160 | tf_op jit(solution)/shard_map/ppermute | solution.py:395
  79.4 0.0 all-to-all-done.3.basis_ref
  79.4 3.4 %collective-permute-done.1.far_ref = bf16[64,128]{1,0:T(8,128)(2,1)S(1)} collective-permute-done((bf16[64,128]{1,0:T(8,128)(2,1)S(1)}, bf16[64,128]{1,0:T(8,128)(2,1)S(1)}, u32[]{:S(2)}, u32[]{:S(2)}) %collective-permute-start.1) | collective-permute-done | bytes 16416 | tf_op jit(solution)/shard_map/ppermute | solution.py:395
  82.9 0.8 shard_map.83
  (1 shorter events, 0.0 us)
Async XLA Ops:
  5.0 13.2 %copy-start = (bf16[8,4,2,8,32]{4,3,2,1,0:T(8,128)(2,1)S(1)}, bf16[8,4,2,8,32]{4,3,2,1,0:T(8,128)(2,1)}, u32[]{:S(2)}) copy-start(bf16[8,4,2,8,32]{4,3,2,1,0:T(8,128)(2,1)} %param.10) | copy-start | bytes 98308
  5.0 37.6 %copy-start.1 = (bf16[2,32,32,256]{3,2,1,0:T(8,128)(2,1)S(1)}, bf16[2,32,32,256]{3,2,1,0:T(8,128)(2,1)}, u32[]{:S(2)}) copy-start(bf16[2,32,32,256]{3,2,1,0:T(8,128)(2,1)} %param.6) | copy-start | bytes 3145732
  5.0 13.2 %all-to-all-start = ((bf16[4,64,512]{2,1,0:T(8,128)(2,1)}), bf16[4,64,512]{2,1,0:T(8,128)(2,1)S(1)}, u32[]{:S(2)}, u32[]{:S(2)}) async-start(bf16[4,64,512]{2,1,0:T(8,128)(2,1)} %get-tuple-element.10), calls=%async_computation | async-start | bytes 524288 | tf_op jit(solution)/shard_map/all_to_all | solution.py:360
  18.4 24.2 %copy-start.3 = (bf16[512,512]{1,0:T(8,128)(2,1)S(1)}, bf16[512,512]{1,0:T(8,128)(2,1)}, u32[]{:S(2)}) copy-start(bf16[512,512]{1,0:T(8,128)(2,1)} %constant.38.clone.dft_hbm.dft_ref) | copy-start | bytes 1572868
  18.4 13.3 %collective-permute-start = (bf16[64,512]{1,0:T(8,128)(2,1)S(1)}, bf16[64,512]{1,0:T(8,128)(2,1)S(1)}, u32[]{:S(2)}, u32[]{:S(2)}) collective-permute-start(bf16[64,512]{1,0:T(8,128)(2,1)S(1)} %shard_map.78.mine_ref), channel_id=1, source_target_pairs={{0,256},{64,320},{128,384},{192,448},{256,0},{320,64},{384,128},{4... | collective-permute-start | bytes 196616 | tf_op jit(solution)/shard_map/ppermute | solution.py:367
  31.7 10.8 %copy-start.2 = (bf16[2,4,32,256]{3,2,1,0:T(8,128)(2,1)S(1)}, bf16[2,4,32,256]{3,2,1,0:T(8,128)(2,1)}, u32[]{:S(2)}) copy-start(bf16[2,4,32,256]{3,2,1,0:T(8,128)(2,1)} %maps_ref.1) | copy-start | bytes 393220
  31.8 10.8 %copy-start.4 = (bf16[80,128]{1,0:T(8,128)(2,1)S(1)}, bf16[80,128]{1,0:T(8,128)(2,1)}, u32[]{:S(2)}) copy-start(bf16[80,128]{1,0:T(8,128)(2,1)} %get-tuple-element.11.tables_ref) | copy-start | bytes 61444
  45.3 17.8 %all-to-all-start.2 = ((bf16[32,40,128]{2,1,0:T(8,128)(2,1)}), bf16[32,40,128]{2,1,0:T(8,128)(2,1)S(1)}, u32[]{:S(2)}, u32[]{:S(2)}) async-start(bf16[32,40,128]{2,1,0:T(8,128)(2,1)} %get-tuple-element.12), calls=%async_computation.2 | async-start | bytes 655360 | tf_op jit(solution)/shard_map/all_to_all | solution.py:383
  52.9 9.6 %collective-permute-start.2 = (f32[8,128]{1,0:T(8,128)S(1)}, f32[8,128]{1,0:T(8,128)S(1)}, u32[]{:S(2)}, u32[]{:S(2)}) collective-permute-start(f32[8,128]{1,0:T(8,128)S(1)} %get-tuple-element.15.refs_0_), channel_id=1, source_target_pairs={{0,256},{64,320},{128,384},{192,448},{256,0},{320,64},{384,128},{4... | collective-permute-start | bytes 12296 | tf_op jit(solution)/shard_map/ppermute | solution.py:384
  63.1 16.3 %all-to-all-start.3 = ((f32[4,8,128]{2,1,0:T(8,128)}), f32[4,8,128]{2,1,0:T(8,128)S(1)}, u32[]{:S(2)}, u32[]{:S(2)}) async-start(f32[4,8,128]{2,1,0:T(8,128)} %shard_map.82), calls=%async_computation.3 | async-start | bytes 32768 | tf_op jit(solution)/shard_map/all_to_all | solution.py:396
  68.5 14.3 %collective-permute-start.1 = (bf16[64,128]{1,0:T(8,128)(2,1)S(1)}, bf16[64,128]{1,0:T(8,128)(2,1)S(1)}, u32[]{:S(2)}, u32[]{:S(2)}) collective-permute-start(bf16[64,128]{1,0:T(8,128)(2,1)S(1)} %get-tuple-element.14), channel_id=1, source_target_pairs={{0,32},{1,33},{2,34},{3,35},{4,36},{5,37},{6,38},{7,39},{8,40},{9,... | collective-permute-start | bytes 49160 | tf_op jit(solution)/shard_map/ppermute | solution.py:395

commit v3 on v2

--- a/solution.py
+++ b/solution.py
@@ -212,19 +212,28 @@
     places = half * quads
     owners = out_ref.shape[0]
     size = places // owners
+    moved = jnp.zeros((places, 8 * rows), F32)
+    for q in range(0, quads, 2):
+        pieces = jnp.concatenate(
+            [
+                jnp.concatenate(
+                    [
+                        g[i * 2 * rows : (i + 1) * 2 * rows, z * half : (z + 1) * half]
+                        for i in (q, q + 1)
+                    ],
+                    axis=1,
+                )
+                for z in range(2)
+                for g in (grad_real, grad_imag)
+            ],
+            axis=0,
+        )
+        row, lane = iota((places, 2 * half), 0), iota((places, 2 * half), 1)
+        chosen = one_hot(row == lane % half * quads + q + lane // half)
+        moved = moved + dot_nt(chosen, pieces)
+    moved = moved.astype(BF16)
     for z in range(2):
-        moved = jnp.zeros((places, 4 * rows), F32)
-        for q in range(quads):
-            piece = jnp.concatenate(
-                [
-                    g[q * 2 * rows : (q + 1) * 2 * rows, z * half : (z + 1) * half]
-                    for g in (grad_real, grad_imag)
-                ],
-                axis=0,
-            )
-            chosen = one_hot(iota((places, half), 0) == iota((places, half), 1) * quads + q)
-            moved = moved + dot_nt(chosen, piece)
-        out_ref[:, z * size : (z + 1) * size, :] = moved.astype(BF16).reshape(
+        out_ref[:, z * size : (z + 1) * size, :] = moved[:, z * 4 * rows : (z + 1) * 4 * rows].reshape(
             owners, size, 4 * rows
         )
     tile = tables_ref[2 * rows : 2 * rows + frames, :]

time: 84.1 us -> 83.9 us (level)
  no operation moved by 1% of the time
where the time goes in v3:
time: 83.9 us; the launch traced here: 83.4 us
  starting transfers between devices  46.9 us (56%)
  waiting for transfers between devices  16.2 us (19%)
  blocking collectives  10.8 us (13%)
  Pallas kernels  8.8 us (10%)
    ppermute x1, starting transfers between devices, steps(): far = lax.ppermute(far, 'frm', swapped(devices, owners))  10.9 us
    all_to_all x1, blocking collectives, steps(): lax.all_to_all(residual, 'vox', 0, 0, tiled=True, axis_index_groups=quads)  10.8 us
    ppermute x1, starting transfers between devices, steps(): other = lax.ppermute(mine, 'vox', swapped(members, quad))  9.23 us
    ppermute x1, starting transfers between devices, steps(): basis_part = lax.ppermute(basis_term, 'vox', swapped(members, quad))  8.02 us
    all_to_all x1, starting transfers between devices, steps(): lax.all_to_all(chunks, 'frm', 0, 0, tiled=True, axis_index_groups=groups)  7.62 us
    all_to_all x1, waiting for transfers between devices, steps(): lax.all_to_all(partial_lines, 'vox', 0, 0, tiled=True, axis_index_groups=...  7.05 us
    all_to_all x1, starting transfers between devices, steps(): lax.all_to_all(partial_lines, 'vox', 0, 0, tiled=True, axis_index_groups=...  6.15 us
    all_to_all x1, starting transfers between devices, steps(): lax.all_to_all(basis_term, 'vox', 0, 0, tiled=True, axis_index_groups=quads)  4.99 us
  transfers between devices with their start and end apart: 6, of which 4 were waited for; matrix products, arithmetic and copies ran while one was open for 0% of the time, Pallas kernels for 1%

profile of v3, /device:TPU:34, one launch (start us, length us, event | category | flops | bytes accessed | tf_op | source)
XLA Modules:
  0.0 83.4 jit_solution(14866188131972209040)
XLA Ops:
  0.6 4.3 %shard_map.77 = (bf16[4,64,512]{2,1,0:T(8,128)(2,1)}, bf16[80,128]{1,0:T(8,128)(2,1)}) custom-call(s32[1]{0:T(128)} %bitcast.2.v_ref, bf16[2,1024,256]{2,1,0:T(8,128)(2,1)} %bitcast.8, bf16[8,32]{1,0:T(8,128)(2,1)} %bitcast.11, bf16[2,4,32,256]{3,2,1,0:T(8,128)(2,1)} %maps_ref.1, s32[8,8]{1,0:T(8,128)} %lines_hbm.1, ...), custom_call_target="tpu_custom_call" | custom-call | flops 2000000000 | bytes 3000000 | tf_op jit(solution)/shard_map/pallas_call | solution.py:353
  5.0 0.0 copy-start
  5.0 0.0 copy-start.1
  5.0 6.1 %all-to-all-start = ((bf16[4,64,512]{2,1,0:T(8,128)(2,1)}), bf16[4,64,512]{2,1,0:T(8,128)(2,1)S(1)}, u32[]{:S(2)}, u32[]{:S(2)}) async-start(bf16[4,64,512]{2,1,0:T(8,128)(2,1)} %get-tuple-element.10), calls=%async_computation | async-start | bytes 524288 | tf_op jit(solution)/shard_map/all_to_all | solution.py:369
  11.2 7.0 %all-to-all-done.parts_ref = bf16[4,64,512]{2,1,0:T(8,128)(2,1)S(1)} async-done(((bf16[4,64,512]{2,1,0:T(8,128)(2,1)}), bf16[4,64,512]{2,1,0:T(8,128)(2,1)S(1)}, u32[]{:S(2)}, u32[]{:S(2)}) %all-to-all-start) | async-done | bytes 262176 | tf_op jit(solution)/shard_map/all_to_all | solution.py:369
  18.2 0.0 copy-done
  18.2 0.2 shard_map.78.mine_ref
  18.4 0.0 copy-start.3
  18.4 9.2 %collective-permute-start = (bf16[64,512]{1,0:T(8,128)(2,1)S(1)}, bf16[64,512]{1,0:T(8,128)(2,1)S(1)}, u32[]{:S(2)}, u32[]{:S(2)}) collective-permute-start(bf16[64,512]{1,0:T(8,128)(2,1)S(1)} %shard_map.78.mine_ref), channel_id=1, source_target_pairs={{0,256},{64,320},{128,384},{192,448},{256,0},{320,64},{384,128},{4... | collective-permute-start | bytes 196616 | tf_op jit(solution)/shard_map/ppermute | solution.py:376
  27.6 4.1 %collective-permute-done.other_ref = bf16[64,512]{1,0:T(8,128)(2,1)S(1)} collective-permute-done((bf16[64,512]{1,0:T(8,128)(2,1)S(1)}, bf16[64,512]{1,0:T(8,128)(2,1)S(1)}, u32[]{:S(2)}, u32[]{:S(2)}) %collective-permute-start) | collective-permute-done | bytes 65568 | tf_op jit(solution)/shard_map/ppermute | solution.py:376
  31.7 0.0 copy-start.2
  31.8 0.0 copy-start.4
  31.8 10.8 %all_to_all.20.res_ref = bf16[4,64,512]{2,1,0:T(8,128)(2,1)S(1)} all-to-all(bf16[4,64,512]{2,1,0:T(8,128)(2,1)S(1)} %shard_map.79), channel_id=1, replica_groups={{0,64,128,192},{256,320,384,448},{1,65,129,193},{257,321,385,449},{2,66..., dimensions={0} | all-to-all | bytes 524288 | tf_op jit(solution)/shard_map/all_to_all | solution.py:380
  42.6 0.0 copy-done.1
  42.6 0.0 copy-done.3
  42.6 0.0 copy-done.2
  42.6 0.0 copy-done.4
  42.6 2.5 %shard_map.80 = (bf16[32,40,128]{2,1,0:T(8,128)(2,1)}, f32[8,128]{1,0:T(8,128)S(1)}) custom-call(bf16[4,64,512]{2,1,0:T(8,128)(2,1)S(1)} %all_to_all.20.res_ref, bf16[2,1024,256]{2,1,0:T(8,128)(2,1)S(1)} %bitcast.9, bf16[2,4,32,256]{3,2,1,0:T(8,128)(2,1)S(1)} %copy-done.2, bf16[80,128]{1,0:T(8,128)(2,1)S(1)} %copy-done.4, bf16[512,512]{1,0:T(8,128)(2,1)S(1)} %copy-done.3), custom_call_target="tpu_custom_call" | custom-call | flops 4000000000 | bytes 3000000 | tf_op jit(solution)/shard_map/pallas_call | solution.py:384
  45.1 7.6 %all-to-all-start.2 = ((bf16[32,40,128]{2,1,0:T(8,128)(2,1)}), bf16[32,40,128]{2,1,0:T(8,128)(2,1)S(1)}, u32[]{:S(2)}, u32[]{:S(2)}) async-start(bf16[32,40,128]{2,1,0:T(8,128)(2,1)} %get-tuple-element.12), calls=%async_computation.2 | async-start | bytes 655360 | tf_op jit(solution)/shard_map/all_to_all | solution.py:392
  52.7 8.0 %collective-permute-start.2 = (f32[8,128]{1,0:T(8,128)S(1)}, f32[8,128]{1,0:T(8,128)S(1)}, u32[]{:S(2)}, u32[]{:S(2)}) collective-permute-start(f32[8,128]{1,0:T(8,128)S(1)} %get-tuple-element.15.refs_0_), channel_id=1, source_target_pairs={{0,256},{64,320},{128,384},{192,448},{256,0},{320,64},{384,128},{4... | collective-permute-start | bytes 12296 | tf_op jit(solution)/shard_map/ppermute | solution.py:393
  60.8 1.6 %collective-permute-done.2.refs_1_ = f32[8,128]{1,0:T(8,128)S(1)} collective-permute-done((f32[8,128]{1,0:T(8,128)S(1)}, f32[8,128]{1,0:T(8,128)S(1)}, u32[]{:S(2)}, u32[]{:S(2)}) %collective-permute-start.2) | collective-permute-done | bytes 4128 | tf_op jit(solution)/shard_map/ppermute | solution.py:393
  62.4 0.6 shard_map.82
  63.0 0.0 all-to-all-done.2.chunks_ref
  63.0 5.0 %all-to-all-start.3 = ((f32[4,8,128]{2,1,0:T(8,128)}), f32[4,8,128]{2,1,0:T(8,128)S(1)}, u32[]{:S(2)}, u32[]{:S(2)}) async-start(f32[4,8,128]{2,1,0:T(8,128)} %shard_map.82), calls=%async_computation.3 | async-start | bytes 32768 | tf_op jit(solution)/shard_map/all_to_all | solution.py:405
  68.0 0.4 shard_map.81
  68.3 10.9 %collective-permute-start.1 = (bf16[64,128]{1,0:T(8,128)(2,1)S(1)}, bf16[64,128]{1,0:T(8,128)(2,1)S(1)}, u32[]{:S(2)}, u32[]{:S(2)}) collective-permute-start(bf16[64,128]{1,0:T(8,128)(2,1)S(1)} %get-tuple-element.14), channel_id=1, source_target_pairs={{0,32},{1,33},{2,34},{3,35},{4,36},{5,37},{6,38},{7,39},{8,40},{9,... | collective-permute-start | bytes 49160 | tf_op jit(solution)/shard_map/ppermute | solution.py:404
  79.2 0.0 all-to-all-done.3.basis_ref
  79.2 3.4 %collective-permute-done.1.far_ref = bf16[64,128]{1,0:T(8,128)(2,1)S(1)} collective-permute-done((bf16[64,128]{1,0:T(8,128)(2,1)S(1)}, bf16[64,128]{1,0:T(8,128)(2,1)S(1)}, u32[]{:S(2)}, u32[]{:S(2)}) %collective-permute-start.1) | collective-permute-done | bytes 16416 | tf_op jit(solution)/shard_map/ppermute | solution.py:404
  82.7 0.8 shard_map.83
  (1 shorter events, 0.0 us)
Async XLA Ops:
  5.0 13.2 %copy-start = (bf16[8,4,2,8,32]{4,3,2,1,0:T(8,128)(2,1)S(1)}, bf16[8,4,2,8,32]{4,3,2,1,0:T(8,128)(2,1)}, u32[]{:S(2)}) copy-start(bf16[8,4,2,8,32]{4,3,2,1,0:T(8,128)(2,1)} %param.10) | copy-start | bytes 98308
  5.0 37.6 %copy-start.1 = (bf16[2,32,32,256]{3,2,1,0:T(8,128)(2,1)S(1)}, bf16[2,32,32,256]{3,2,1,0:T(8,128)(2,1)}, u32[]{:S(2)}) copy-start(bf16[2,32,32,256]{3,2,1,0:T(8,128)(2,1)} %param.6) | copy-start | bytes 3145732
  5.0 13.2 %all-to-all-start = ((bf16[4,64,512]{2,1,0:T(8,128)(2,1)}), bf16[4,64,512]{2,1,0:T(8,128)(2,1)S(1)}, u32[]{:S(2)}, u32[]{:S(2)}) async-start(bf16[4,64,512]{2,1,0:T(8,128)(2,1)} %get-tuple-element.10), calls=%async_computation | async-start | bytes 524288 | tf_op jit(solution)/shard_map/all_to_all | solution.py:369
  18.4 24.2 %copy-start.3 = (bf16[512,512]{1,0:T(8,128)(2,1)S(1)}, bf16[512,512]{1,0:T(8,128)(2,1)}, u32[]{:S(2)}) copy-start(bf16[512,512]{1,0:T(8,128)(2,1)} %constant.38.clone.dft_hbm.dft_ref) | copy-start | bytes 1572868
  18.4 13.3 %collective-permute-start = (bf16[64,512]{1,0:T(8,128)(2,1)S(1)}, bf16[64,512]{1,0:T(8,128)(2,1)S(1)}, u32[]{:S(2)}, u32[]{:S(2)}) collective-permute-start(bf16[64,512]{1,0:T(8,128)(2,1)S(1)} %shard_map.78.mine_ref), channel_id=1, source_target_pairs={{0,256},{64,320},{128,384},{192,448},{256,0},{320,64},{384,128},{4... | collective-permute-start | bytes 196616 | tf_op jit(solution)/shard_map/ppermute | solution.py:376
  31.7 10.8 %copy-start.2 = (bf16[2,4,32,256]{3,2,1,0:T(8,128)(2,1)S(1)}, bf16[2,4,32,256]{3,2,1,0:T(8,128)(2,1)}, u32[]{:S(2)}) copy-start(bf16[2,4,32,256]{3,2,1,0:T(8,128)(2,1)} %maps_ref.1) | copy-start | bytes 393220
  31.8 10.8 %copy-start.4 = (bf16[80,128]{1,0:T(8,128)(2,1)S(1)}, bf16[80,128]{1,0:T(8,128)(2,1)}, u32[]{:S(2)}) copy-start(bf16[80,128]{1,0:T(8,128)(2,1)} %get-tuple-element.11.tables_ref) | copy-start | bytes 61444
  45.1 17.8 %all-to-all-start.2 = ((bf16[32,40,128]{2,1,0:T(8,128)(2,1)}), bf16[32,40,128]{2,1,0:T(8,128)(2,1)S(1)}, u32[]{:S(2)}, u32[]{:S(2)}) async-start(bf16[32,40,128]{2,1,0:T(8,128)(2,1)} %get-tuple-element.12), calls=%async_computation.2 | async-start | bytes 655360 | tf_op jit(solution)/shard_map/all_to_all | solution.py:392
  52.7 9.6 %collective-permute-start.2 = (f32[8,128]{1,0:T(8,128)S(1)}, f32[8,128]{1,0:T(8,128)S(1)}, u32[]{:S(2)}, u32[]{:S(2)}) collective-permute-start(f32[8,128]{1,0:T(8,128)S(1)} %get-tuple-element.15.refs_0_), channel_id=1, source_target_pairs={{0,256},{64,320},{128,384},{192,448},{256,0},{320,64},{384,128},{4... | collective-permute-start | bytes 12296 | tf_op jit(solution)/shard_map/ppermute | solution.py:393
  63.0 16.3 %all-to-all-start.3 = ((f32[4,8,128]{2,1,0:T(8,128)}), f32[4,8,128]{2,1,0:T(8,128)S(1)}, u32[]{:S(2)}, u32[]{:S(2)}) async-start(f32[4,8,128]{2,1,0:T(8,128)} %shard_map.82), calls=%async_computation.3 | async-start | bytes 32768 | tf_op jit(solution)/shard_map/all_to_all | solution.py:405
  68.3 14.3 %collective-permute-start.1 = (bf16[64,128]{1,0:T(8,128)(2,1)S(1)}, bf16[64,128]{1,0:T(8,128)(2,1)S(1)}, u32[]{:S(2)}, u32[]{:S(2)}) collective-permute-start(bf16[64,128]{1,0:T(8,128)(2,1)S(1)} %get-tuple-element.14), channel_id=1, source_target_pairs={{0,32},{1,33},{2,34},{3,35},{4,36},{5,37},{6,38},{7,39},{8,40},{9,... | collective-permute-start | bytes 49160 | tf_op jit(solution)/shard_map/ppermute | solution.py:404
